TPU v7x, 256 devices: a whole 4x4x8 slice. The times are simulated.
256 devices in a mesh: wide: 64 (over y, z, core), narrow: 4 (over x).
Axes of the slice: x: 4, y: 4, z: 8, core: 2. Of those that a mesh axis runs over, the one named last changes fastest.
Arguments:
- patches: bfloat16 [65536, 1280], P('wide', 'narrow'), may hold values from -6 to 6
- norm_gain: float32 [1280], replicated, may hold values from 0.1 to 1.9
- norm_bias: float32 [1280], replicated, may hold values from -3 to 3
- w_in: bfloat16 [1280, 5120], P('wide', 'narrow'), may hold values from -0.15625 to 0.15625
- b_in: float32 [5120], P('narrow'), may hold values from -3 to 3
- w_out: bfloat16 [5120, 1280], P('narrow', 'wide'), may hold values from -0.078125 to 0.078125
- b_out: float32 [1280], P('narrow'), may hold values from -3 to 3
- w_proj: bfloat16 [4, 1280, 1280], P(None, 'narrow', 'wide'), may hold values from -0.078125 to 0.078125
- b_proj: float32 [1280], P('narrow'), may hold values from -3 to 3
- text: bfloat16 [32768, 1280], P('wide', 'narrow'), may hold values from -6 to 6
- place: int32 [16384], replicated, may hold values from -1 to 32767, as said below
Outputs:
- prompt_embeds: bfloat16 [32768, 1280], P('wide', 'narrow')
Inputs may be any that keep to these rules, and one draw needn't show every extreme that they name: `place`: of the 256 entries of one wide index (entries i * 256 to (i + 1) * 256 - 1), the valid ones (>= 0) come first and -1 fills the rest; three quarters or more are valid, and all are valid for some wide index. Valid values are distinct. For one wide index, at most 8 valid entries v have the same v // 512, and every wide index reaches 8 for some value.
All inputs are finite; a program needn't handle non-finite values.
Results may differ from a plain program's by a relative error of at most 0.012.
Values may be sent and summed in bfloat16 or wider, within the bound.
A program may use at most 64 MiB of HBM per device.

v0:
```python
import jax
import jax.numpy as jnp
from jax import lax
from jax.sharding import PartitionSpec as P


def select_rows(index, rows, count):
    pick = (jnp.arange(count, dtype=jnp.int32)[:, None] == index[None, :]).astype(rows.dtype)
    return jnp.dot(pick, rows, preferred_element_type=jnp.float32).astype(rows.dtype)


def per_device(
    patches, norm_gain, norm_bias, w_in, b_in, w_out, b_out, w_proj, b_proj, text, place
):
    groups = lax.axis_size("wide")
    width = w_in.shape[0]
    local = jnp.concatenate([w_in, w_out.T, w_proj.transpose(2, 0, 1).reshape(width, -1)], axis=0)
    gathered = lax.all_gather(local, "wide", axis=0, tiled=False)
    rows_in = gathered[:, :width].reshape(groups * width, -1)
    cols_out = gathered[:, width : 2 * width].reshape(groups * width, -1)
    proj_cols = gathered[:, 2 * width :].reshape(groups * width, -1)
    whole = lax.all_gather(patches, "narrow", axis=1, tiled=True)
    values = whole.astype(jnp.float32)
    center = jnp.mean(values, axis=-1, keepdims=True)
    spread = jnp.mean(jnp.square(values - center), axis=-1, keepdims=True)
    normed = ((values - center) * lax.rsqrt(spread + 1e-06) * norm_gain + norm_bias).astype(
        jnp.bfloat16
    )
    product = jnp.dot(normed, rows_in, preferred_element_type=jnp.float32)
    hidden = jax.nn.gelu(product + b_in, approximate=False).astype(jnp.bfloat16)
    partial_out = lax.dot_general(
        hidden, cols_out, (((1,), (1,)), ((), ())), preferred_element_type=jnp.float32
    )
    mlp_out = lax.psum_scatter(
        partial_out.astype(jnp.bfloat16), "narrow", scatter_dimension=1, tiled=True
    ).astype(jnp.float32)
    stream = (patches.astype(jnp.float32) + (mlp_out + b_out)).astype(jnp.bfloat16)
    merge_count = stream.shape[0] // 4
    merged = stream.reshape(merge_count, 4 * stream.shape[1])
    own_index = lax.axis_index("wide")
    seq_rows = text.shape[0]
    bucket = seq_rows // groups
    place_table = place.reshape(groups, merge_count)
    owners = jnp.where(place_table >= 0, place_table // seq_rows, groups)
    own_owners = lax.dynamic_index_in_dim(owners, own_index, 0, keepdims=False)
    owner_hits = (own_owners[:, None] == jnp.arange(groups, dtype=jnp.int32)[None, :]).astype(
        jnp.int32
    )
    slot_out = jnp.sum(jnp.cumsum(owner_hits, axis=0) * owner_hits, axis=1) - 1
    send_row = jnp.where(
        (own_owners < groups) & (slot_out < bucket), own_owners * bucket + slot_out, -1
    )
    arriving = owners == own_index
    slot_in = jnp.cumsum(arriving.astype(jnp.int32), axis=1) - 1
    slot_in = jnp.where(arriving, slot_in, bucket)
    local_row = place_table % seq_rows
    slot_hits = slot_in[:, :, None] == jnp.arange(bucket, dtype=jnp.int32)[None, None, :]
    targets = jnp.sum(jnp.where(slot_hits, local_row[:, :, None] + 1, 0), axis=1) - 1
    partial_proj = lax.dot_general(
        merged, proj_cols, (((1,), (1,)), ((), ())), preferred_element_type=jnp.float32
    )
    vision = (
        lax.psum_scatter(
            partial_proj.astype(jnp.bfloat16), "narrow", scatter_dimension=1, tiled=True
        ).astype(jnp.float32)
        + b_proj
    ).astype(jnp.bfloat16)
    outgoing = select_rows(send_row, vision, groups * bucket).reshape(groups, bucket, -1)
    received = lax.all_to_all(outgoing, "wide", split_axis=0, concat_axis=0, tiled=True)
    flat_targets = targets.reshape(-1)
    placed = select_rows(flat_targets, received.reshape(-1, received.shape[2]), seq_rows)
    hit = jnp.any(jnp.arange(seq_rows, dtype=jnp.int32)[:, None] == flat_targets[None, :], axis=1)
    return jnp.where(hit[:, None], placed, text)


def solution(mesh):
    placed = (
        P("wide", "narrow"),
        P(),
        P(),
        P("wide", "narrow"),
        P("narrow"),
        P("narrow", "wide"),
        P("narrow"),
        P(None, "narrow", "wide"),
        P("narrow"),
        P("wide", "narrow"),
        P(),
    )
    return jax.shard_map(
        per_device, mesh=mesh, in_specs=placed, out_specs=P("wide", "narrow"), check_vma=False
    )
```

profile of v0, /device:TPU:1, one launch (start us, length us, event | category | flops | bytes accessed | tf_op | source)
XLA Modules:
  0.0 286.6 jit_solution(14069685264983872683)
XLA Ops:
  6.5 0.0 all-gather.5.cloned.1.call-start
  6.5 0.7 all-gather.5.cloned.1.call-update
  7.3 0.0 all-gather.7.cloned.1.call-start
  7.3 0.9 reshape.177
  8.2 1.6 maximum_bitcast_fusion
  9.8 0.0 all-gather.7.cloned.1.call-update
  9.8 0.0 reduce-scatter.5.cloned.1.call-start
  9.9 40.8 %all-gather.5.cloned.1.call-done = bf16[1024,1280]{0,1:T(8,128)(2,1)} async-done(((bf16[1024,320]{0,1:T(8,128)(2,1)}), bf16[1024,1280]{0,1:T(8,128)(2,1)}) %all-gather.5.cloned.1.call-update) | async-done | bytes 2621456 | tf_op jit(solution)/shard_map/all_gather | solution.py:22
  50.7 2.2 convert_reduce_fusion
  52.9 2.5 fusion.2
  55.4 85.1 %all-gather.7.cloned.1.call-done = bf16[64,60,1280]{2,1,0:T(8,128)(2,1)} async-done(((bf16[1,60,1280]{2,1,0:T(8,128)(2,1)}), bf16[64,60,1280]{2,1,0:T(8,128)(2,1)}) %all-gather.7.cloned.1.call-update) | async-done | bytes 9830416 | tf_op jit(solution)/shard_map/all_gather | solution.py:18
  140.5 8.2 %fusion.72 = (bf16[64,20,1280]{2,1,0:T(8,128)(2,1)}, bf16[64,20,1280]{2,1,0:T(8,128)(2,1)}, bf16[64,20,1280]{2,1,0:T(8,128)(2,1)}) fusion(bf16[64,60,1280]{2,1,0:T(8,128)(2,1)} %all-gather.7.cloned.1.call-done), kind=kLoop, calls=%fused_computation.116 | loop fusion | bytes 19660800 | tf_op jit(solution)/shard_map/slice | solution.py:21
  148.7 6.1 %reshape.179 = bf16[1280,1280]{1,0:T(8,128)(2,1)} reshape(bf16[64,20,1280]{2,1,0:T(8,128)(2,1)} %get-tuple-element.6) | data formatting | bytes 6553600 | tf_op jit(solution)/shard_map/reshape | solution.py:20
  154.9 6.3 %reshape.178 = bf16[1280,1280]{1,0:T(8,128)(2,1)} reshape(bf16[64,20,1280]{2,1,0:T(8,128)(2,1)} %get-tuple-element.7) | data formatting | bytes 6553600 | tf_op jit(solution)/shard_map/reshape | solution.py:19
  161.2 0.0 copy-done
  161.2 0.0 copy-done.3
  161.2 0.0 copy-done.4
  161.2 0.0 copy-done.5
  161.2 0.0 copy-start.1
  161.2 21.5 %convolution_convert_fusion = bf16[1024,1280]{0,1:T(8,128)(2,1)} fusion(bf16[1280,1280]{1,0:T(8,128)(2,1)} %reshape.179, bf16[1280,1280]{1,0:T(8,128)(2,1)} %reshape.178, bf16[1024,1280]{0,1:T(8,128)(2,1)S(1)} %copy-done, f32[1280]{0:T(1024)S(1)} %copy-done.3, f32[1280]{0:T(1024)S(1)} %copy-done.4, f32[1280]{0:T(1024)S(1)} %copy-done.5, ...), kind=kOutput, calls=%fused_computation.27 | convolution fusion | flops 6806568960 | bytes 11820032 | tf_op jit(solution)/shard_map/dot_general | solution.py:31
  182.7 0.0 reduce-scatter.5.cloned.1.call-update
  182.7 0.0 reduce-scatter.7.cloned.1.call-start
  182.8 0.0 copy-done.1
  182.8 0.1 fusion.40
  182.9 0.6 reduce-window.14
  183.5 4.6 %reshape.181 = bf16[1280,1280]{1,0:T(8,128)(2,1)S(1)} reshape(bf16[64,20,1280]{2,1,0:T(8,128)(2,1)} %get-tuple-element.5) | data formatting | bytes 6553600 | tf_op jit(solution)/shard_map/reshape | solution.py:21
  188.1 27.8 %reduce-scatter.5.cloned.1.call-done = bf16[1024,320]{0,1:T(8,128)(2,1)} async-done(((bf16[1024,1280]{0,1:T(8,128)(2,1)}), bf16[1024,320]{0,1:T(8,128)(2,1)}) %reduce-scatter.5.cloned.1.call-update) | async-done | bytes 655376 | tf_op jit(solution)/shard_map/reduce_scatter | solution.py:34
  215.9 0.0 copy-done.2
  215.9 2.4 add_convert_fusion
  218.3 2.2 copy.38
  220.5 2.5 reshape.180
  223.0 3.0 %fusion.21 = bf16[1280,256]{1,0:T(8,128)(2,1)} fusion(bf16[256,1280]{1,0:T(8,128)(2,1)} %reshape.180, bf16[1280,1280]{1,0:T(8,128)(2,1)S(1)} %reshape.181), kind=kOutput, calls=%fused_computation.33 | convolution fusion | flops 839188480 | bytes 4587520 | tf_op jit(solution)/shard_map/dot_general | solution.py:59
  226.0 0.0 reduce-scatter.7.cloned.1.call-update
  226.0 0.2 slice_reduce_fusion.1
  226.3 0.1 fusion.30
  226.4 0.6 reduce-window.16
  227.0 0.2 slice_reduce_fusion
  227.2 0.1 fusion.36
  227.4 21.8 %reduce-scatter.7.cloned.1.call-done = bf16[320,256]{1,0:T(8,128)(2,1)} async-done(((bf16[1280,256]{1,0:T(8,128)(2,1)}), bf16[320,256]{1,0:T(8,128)(2,1)}) %reduce-scatter.7.cloned.1.call-update) | async-done | bytes 163856
  249.1 1.1 copy.42
  250.2 0.3 convolution_convert_fusion.2
  250.6 0.9 copy.40
  251.5 11.8 %all-to-all-start = ((bf16[64,8,320]{2,1,0:T(8,128)(2,1)}), bf16[64,8,320]{2,1,0:T(8,128)(2,1)S(1)}, u32[]{:S(2)}, u32[]{:S(2)}) async-start(bf16[64,8,320]{2,1,0:T(8,128)(2,1)} %bitcast.9), calls=%async_computation.1 | async-start | bytes 786432 | tf_op jit(solution)/shard_map/all_to_all | solution.py:69
  263.3 1.2 select_reduce_fusion
  264.5 0.1 sub.43
  264.6 0.2 fusion.25
  264.8 13.2 %all-to-all-done = bf16[64,8,320]{2,1,0:T(8,128)(2,1)S(1)} async-done(((bf16[64,8,320]{2,1,0:T(8,128)(2,1)}), bf16[64,8,320]{2,1,0:T(8,128)(2,1)S(1)}, u32[]{:S(2)}, u32[]{:S(2)}) %all-to-all-start) | async-done | bytes 327712 | tf_op jit(solution)/shard_map/all_to_all | solution.py:69
  277.9 2.1 fusion.24
  (19 shorter events, 0.2 us)
Async XLA Ops:
  6.5 44.2 %all-gather.5.cloned.1.call-start = ((), (), s32[]{:S(2)}) async-start(), calls=%async_computation.3 | async-start | bytes 3276800 | tf_op jit(solution)/shard_map/all_gather | solution.py:22
  7.3 133.2 %all-gather.7.cloned.1.call-start = ((), (), s32[]{:S(2)}) async-start(), calls=%async_computation.5 | async-start | bytes 10649600 | tf_op jit(solution)/shard_map/all_gather | solution.py:18
  9.8 206.1 %reduce-scatter.5.cloned.1.call-start = ((), (), s32[]{:S(2)}) async-start(), calls=%async_computation.4 | async-start | bytes 3276800 | tf_op jit(solution)/shard_map/reduce_scatter | solution.py:34
  154.9 6.3 %copy-start = (bf16[1024,1280]{0,1:T(8,128)(2,1)S(1)}, bf16[1024,1280]{0,1:T(8,128)(2,1)}, u32[]{:S(2)}) copy-start(bf16[1024,1280]{0,1:T(8,128)(2,1)} %all-gather.5.cloned.1.call-done) | copy-start | bytes 7864324
  154.9 6.3 %copy-start.3 = (f32[1280]{0:T(1024)S(1)}, f32[1280]{0:T(1024)}, u32[]{:S(2)}) copy-start(f32[1280]{0:T(1024)} %param.15) | copy-start | bytes 15364
  154.9 6.3 %copy-start.4 = (f32[1280]{0:T(1024)S(1)}, f32[1280]{0:T(1024)}, u32[]{:S(2)}) copy-start(f32[1280]{0:T(1024)} %param.13) | copy-start | bytes 15364
  154.9 6.3 %copy-start.5 = (f32[1280]{0:T(1024)S(1)}, f32[1280]{0:T(1024)}, u32[]{:S(2)}) copy-start(f32[1280]{0:T(1024)} %param.12) | copy-start | bytes 15364
  161.2 21.6 %copy-start.1 = (s32[16384]{0:T(1024)S(1)}, s32[16384]{0:T(1024)}, u32[]{:S(2)}) copy-start(s32[16384]{0:T(1024)} %param.21) | copy-start | bytes 196612
  182.7 33.2 %copy-start.2 = (f32[320]{0:T(512)S(1)}, f32[320]{0:T(512)}, u32[]{:S(2)}) copy-start(f32[320]{0:T(512)} %param.17) | copy-start | bytes 3844
  182.7 66.4 %reduce-scatter.7.cloned.1.call-start = ((), (), s32[]{:S(2)}) async-start(), calls=%async_computation.6 | async-start | bytes 819200
  218.3 31.9 %copy-start.6 = (f32[320]{0:T(512)S(1)}, f32[320]{0:T(512)}, u32[]{:S(2)}) copy-start(f32[320]{0:T(512)} %param.19) | copy-start | bytes 3844
  251.5 26.4 %all-to-all-start = ((bf16[64,8,320]{2,1,0:T(8,128)(2,1)}), bf16[64,8,320]{2,1,0:T(8,128)(2,1)S(1)}, u32[]{:S(2)}, u32[]{:S(2)}) async-start(bf16[64,8,320]{2,1,0:T(8,128)(2,1)} %bitcast.9), calls=%async_computation.1 | async-start | bytes 786432 | tf_op jit(solution)/shard_map/all_to_all | solution.py:69
Sparse Core Ops, SparseCore 0:
  9.2 41.5 all-gather.4
  53.5 86.9 all-gather.6
  182.8 33.0 reduce-scatter.4
  226.2 22.9 reduce-scatter.6
where the time goes:
time: 287 us
  waiting for transfers between devices  189 us (66%)
  local copies, waits for them, and re-layouts  33.5 us (12%)
  matrix products  26.9 us (9%)
  between operations  13.3 us (5%)
  starting transfers between devices  12 us (4%)
  other arithmetic  11.6 us (4%)
    all_gather x1, waiting for transfers between devices, per_device(): gathered = lax.all_gather(local, 'wide', axis=0, tiled=False)  85.1 us
    all_gather x1, waiting for transfers between devices, per_device(): whole = lax.all_gather(patches, 'narrow', axis=1, tiled=True)  40.8 us
    reduce_scatter x1, waiting for transfers between devices, per_device(): lax.psum_scatter(partial_out.astype(jnp.bfloat16), 'narrow', scatter_dime...  27.8 us
    unnamed x5, waiting for transfers between devices  22.5 us
    dot_general x1, matrix products, per_device(): lax.dot_general(hidden, cols_out, (((1,), (1,)), ((), ())), preferred_ele...  21.5 us
    all_to_all x1, waiting for transfers between devices, per_device(): lax.all_to_all(outgoing, 'wide', split_axis=0, concat_axis=0, tiled=True)  13.2 us
    all_to_all x1, starting transfers between devices, per_device(): lax.all_to_all(outgoing, 'wide', split_axis=0, concat_axis=0, tiled=True)  11.8 us
    slice x1, local copies, waits for them, and re-layouts, per_device(): proj_cols = gathered[:, 2 * width:].reshape(groups * width, -1)  8.25 us
  transfers between devices with their start and end apart: 5, of which 5 were waited for; matrix products, arithmetic and copies ran while one was open for 5% of the time, Pallas kernels for 0%

commit v1 on v0

--- a/solution.py
+++ b/solution.py
@@ -19,7 +19,11 @@
     rows_in = gathered[:, :width].reshape(groups * width, -1)
     cols_out = gathered[:, width : 2 * width].reshape(groups * width, -1)
     proj_cols = gathered[:, 2 * width :].reshape(groups * width, -1)
-    whole = lax.all_gather(patches, "narrow", axis=1, tiled=True)
+    size = lax.axis_size("narrow")
+    repeats = [size if d == 1 else 1 for d in range(patches.ndim)]
+    whole = lax.all_to_all(
+        jnp.tile(patches, repeats), "narrow", split_axis=1, concat_axis=1, tiled=True
+    )
     values = whole.astype(jnp.float32)
     center = jnp.mean(values, axis=-1, keepdims=True)
     spread = jnp.mean(jnp.square(values - center), axis=-1, keepdims=True)

time: 287 us -> 245 us (0.85)
  waiting for transfers between devices: 189 us -> 143 us
  starting transfers between devices: 12 us -> 17 us
    all_gather x1 -> x0, waiting for transfers between devices: 40.8 us -> none  [per_device(): whole = lax.all_gather(patches, 'narrow', axis=1, tiled=True)]
    all_gather x1, waiting for transfers between devices: 85.1 us -> 50.6 us  [per_device(): gathered = lax.all_gather(local, 'wide', axis=0, tiled=False)]
    all_to_all x0 -> x1, waiting for transfers between devices: none -> 29.8 us  [per_device(): lax.all_to_all(jnp.tile(patches, repeats), 'narrow', split_axis=1, concat...]
    all_to_all x0 -> x1, starting transfers between devices: none -> 4.84 us  [per_device(): lax.all_to_all(jnp.tile(patches, repeats), 'narrow', split_axis=1, concat...]
    another operation x3 -> x4, local copies, waits for them, and re-layouts: 0.19 us -> 3.13 us  [the longest x1 2.94 us: per_device(): jnp.tile(patches, repeats)]
    unnamed x5 -> x4, waiting for transfers between devices: 22.5 us -> 21.7 us
  transfers between devices with their start and end apart: 5 -> 5, of which waited for: 5 -> 5; matrix products, arithmetic and copies ran while one was open for 5% -> 6% of each run, Pallas kernels for 0% -> 0%
where the time goes in v1:
time: 245 us; the launch traced here: 244 us
  waiting for transfers between devices  143 us (58%)
  local copies, waits for them, and re-layouts  35 us (14%)
  matrix products  25.8 us (11%)
  starting transfers between devices  17 us (7%)
  between operations  13.3 us (5%)
  other arithmetic  10.2 us (4%)
    all_gather x1, waiting for transfers between devices, per_device(): gathered = lax.all_gather(local, 'wide', axis=0, tiled=False)  50.6 us
    all_to_all x1, waiting for transfers between devices, per_device(): lax.all_to_all(jnp.tile(patches, repeats), 'narrow', split_axis=1, concat...  29.8 us
    reduce_scatter x1, waiting for transfers between devices, per_device(): lax.psum_scatter(partial_out.astype(jnp.bfloat16), 'narrow', scatter_dime...  27.6 us
    unnamed x4, waiting for transfers between devices  21.7 us
    dot_general x1, matrix products, per_device(): lax.dot_general(hidden, cols_out, (((1,), (1,)), ((), ())), preferred_ele...  20.4 us
    all_to_all x1, waiting for transfers between devices, per_device(): lax.all_to_all(outgoing, 'wide', split_axis=0, concat_axis=0, tiled=True)  13.2 us
    all_to_all x1, starting transfers between devices, per_device(): lax.all_to_all(outgoing, 'wide', split_axis=0, concat_axis=0, tiled=True)  11.9 us
    slice x1, local copies, waits for them, and re-layouts, per_device(): proj_cols = gathered[:, 2 * width:].reshape(groups * width, -1)  8.25 us
  transfers between devices with their start and end apart: 5, of which 5 were waited for; matrix products, arithmetic and copies ran while one was open for 6% of the time, Pallas kernels for 0%

profile of v1, /device:TPU:1, one launch (start us, length us, event | category | flops | bytes accessed | tf_op | source)
XLA Modules:
  0.0 244.1 jit_solution(5724253733131913061)
XLA Ops:
  6.5 0.0 all-gather.4.cloned.1.call-start
  6.5 1.0 reshape.210
  7.5 1.6 maximum_bitcast_fusion
  9.1 0.0 all-gather.4.cloned.1.call-update
  9.1 2.9 %tile.2 = bf16[1024,4,320]{0,2,1:T(8,128)(2,1)} broadcast(bf16[1024,320]{0,1:T(8,128)(2,1)} %param.11), dimensions={0,2} | broadcast | bytes 3276800 | tf_op jit(solution)/shard_map/tile | solution.py:25
  12.0 4.8 %all-to-all-start = ((bf16[1024,4,320]{0,2,1:T(8,128)(2,1)}), bf16[1024,4,320]{0,2,1:T(8,128)(2,1)S(1)}, u32[]{:S(2)}, u32[]{:S(2)}) async-start(bf16[1024,4,320]{0,2,1:T(8,128)(2,1)} %tile.2), calls=%async_computation | async-start | bytes 5242880 | tf_op jit(solution)/shard_map/all_to_all | solution.py:24
  16.9 0.0 reduce-scatter.5.cloned.1.call-start
  16.9 0.0 copy-done.1
  16.9 0.1 add.116
  17.0 0.0 copy-done.2
  17.0 0.1 mul.46
  17.0 29.8 %all-to-all-done = bf16[1024,4,320]{0,2,1:T(8,128)(2,1)S(1)} async-done(((bf16[1024,4,320]{0,2,1:T(8,128)(2,1)}), bf16[1024,4,320]{0,2,1:T(8,128)(2,1)S(1)}, u32[]{:S(2)}, u32[]{:S(2)}) %all-to-all-start) | async-done | bytes 2621472 | tf_op jit(solution)/shard_map/all_to_all | solution.py:24
  46.8 0.5 convert_reduce_fusion
  47.3 0.7 fusion.2
  48.0 2.1 fusion.5
  50.2 50.6 %all-gather.4.cloned.1.call-done = bf16[64,60,1280]{2,1,0:T(8,128)(2,1)} async-done(((bf16[1,60,1280]{2,1,0:T(8,128)(2,1)}), bf16[64,60,1280]{2,1,0:T(8,128)(2,1)}) %all-gather.4.cloned.1.call-update) | async-done | bytes 9830416 | tf_op jit(solution)/shard_map/all_gather | solution.py:18
  100.8 8.2 %fusion.65 = (bf16[64,20,1280]{2,1,0:T(8,128)(2,1)}, bf16[64,20,1280]{2,1,0:T(8,128)(2,1)}, bf16[64,20,1280]{2,1,0:T(8,128)(2,1)}) fusion(bf16[64,60,1280]{2,1,0:T(8,128)(2,1)} %all-gather.4.cloned.1.call-done), kind=kLoop, calls=%fused_computation.112 | loop fusion | bytes 19660800 | tf_op jit(solution)/shard_map/slice | solution.py:21
  109.1 4.6 %reshape.212 = bf16[1280,1280]{1,0:T(8,128)(2,1)S(1)} reshape(bf16[64,20,1280]{2,1,0:T(8,128)(2,1)} %get-tuple-element.6) | data formatting | bytes 6553600 | tf_op jit(solution)/shard_map/reshape | solution.py:20
  113.7 0.0 copy-start.4
  113.7 6.1 %reshape.211 = bf16[1280,1280]{1,0:T(8,128)(2,1)} reshape(bf16[64,20,1280]{2,1,0:T(8,128)(2,1)} %get-tuple-element.7) | data formatting | bytes 6553600 | tf_op jit(solution)/shard_map/reshape | solution.py:19
  119.8 0.0 copy-done.4
  119.8 20.4 %convolution_convert_fusion = bf16[1024,1280]{0,1:T(8,128)(2,1)} fusion(bf16[1280,1280]{1,0:T(8,128)(2,1)S(1)} %reshape.212, bf16[1024,1280]{0,1:T(8,128)(2,1)} %bitcast.42, bf16[1280,1280]{1,0:T(8,128)(2,1)} %reshape.211, f32[1280]{0:T(1024)S(1)} %copy-done.4), kind=kOutput, calls=%fused_computation.27 | convolution fusion | flops 6798704640 | bytes 11801600 | tf_op jit(solution)/shard_map/dot_general | solution.py:35
  140.2 0.0 reduce-scatter.5.cloned.1.call-update
  140.2 0.2 reduce-scatter.7.cloned.1.call-start
  140.5 0.1 fusion.33
  140.6 0.6 reduce-window.14
  141.2 4.6 %reshape.214 = bf16[1280,1280]{1,0:T(8,128)(2,1)S(1)} reshape(bf16[64,20,1280]{2,1,0:T(8,128)(2,1)} %get-tuple-element.5) | data formatting | bytes 6553600 | tf_op jit(solution)/shard_map/reshape | solution.py:21
  145.8 27.6 %reduce-scatter.5.cloned.1.call-done = bf16[1024,320]{0,1:T(8,128)(2,1)} async-done(((bf16[1024,1280]{0,1:T(8,128)(2,1)}), bf16[1024,320]{0,1:T(8,128)(2,1)}) %reduce-scatter.5.cloned.1.call-update) | async-done | bytes 655376 | tf_op jit(solution)/shard_map/reduce_scatter | solution.py:38
  173.5 2.4 add_convert_fusion
  175.8 2.2 copy.39
  178.1 2.5 %reshape.213 = bf16[256,1280]{1,0:T(8,128)(2,1)} reshape(bf16[1024,320]{1,0:T(8,128)(2,1)} %copy.39) | data formatting | bytes 1310720 | tf_op jit(solution)/shard_map/reshape | solution.py:43
  180.6 3.0 %fusion.16 = bf16[1280,256]{1,0:T(8,128)(2,1)} fusion(bf16[256,1280]{1,0:T(8,128)(2,1)} %reshape.213, bf16[1280,1280]{1,0:T(8,128)(2,1)S(1)} %reshape.214), kind=kOutput, calls=%fused_computation.29 | convolution fusion | flops 839188480 | bytes 4587520 | tf_op jit(solution)/shard_map/dot_general | solution.py:63
  183.6 0.0 reduce-scatter.7.cloned.1.call-update
  183.6 0.2 slice_reduce_fusion.1
  183.8 0.1 fusion.23
  183.9 0.6 reduce-window.16
  184.6 0.2 slice_reduce_fusion
  184.8 0.1 fusion.29
  184.9 21.7 %reduce-scatter.7.cloned.1.call-done = bf16[320,256]{1,0:T(8,128)(2,1)} async-done(((bf16[1280,256]{1,0:T(8,128)(2,1)}), bf16[320,256]{1,0:T(8,128)(2,1)}) %reduce-scatter.7.cloned.1.call-update) | async-done | bytes 163856
  206.6 1.1 copy.43
  207.7 0.3 convolution_convert_fusion.2
  208.1 0.9 copy.41
  209.0 11.9 %all-to-all-start.1 = ((bf16[64,8,320]{2,1,0:T(8,128)(2,1)}), bf16[64,8,320]{2,1,0:T(8,128)(2,1)S(1)}, u32[]{:S(2)}, u32[]{:S(2)}) async-start(bf16[64,8,320]{2,1,0:T(8,128)(2,1)} %bitcast.10), calls=%async_computation.2 | async-start | bytes 786432 | tf_op jit(solution)/shard_map/all_to_all | solution.py:73
  220.9 1.2 select_reduce_fusion
  222.0 0.1 sub.45
  222.1 0.2 fusion.18
  222.3 13.2 %all-to-all-done.1 = bf16[64,8,320]{2,1,0:T(8,128)(2,1)S(1)} async-done(((bf16[64,8,320]{2,1,0:T(8,128)(2,1)}), bf16[64,8,320]{2,1,0:T(8,128)(2,1)S(1)}, u32[]{:S(2)}, u32[]{:S(2)}) %all-to-all-start.1) | async-done | bytes 327712 | tf_op jit(solution)/shard_map/all_to_all | solution.py:73
  235.5 2.1 fusion.17
  (20 shorter events, 0.2 us)
Async XLA Ops:
  6.5 10.3 %copy-start.1 = (f32[1280]{0:T(1024)S(1)}, f32[1280]{0:T(1024)}, u32[]{:S(2)}) copy-start(f32[1280]{0:T(1024)} %param.13) | copy-start | bytes 15364
  6.5 10.4 %copy-start.2 = (f32[1280]{0:T(1024)S(1)}, f32[1280]{0:T(1024)}, u32[]{:S(2)}) copy-start(f32[1280]{0:T(1024)} %param.12) | copy-start | bytes 15364
  6.5 94.3 %all-gather.4.cloned.1.call-start = ((), (), s32[]{:S(2)}) async-start(), calls=%async_computation.5 | async-start | bytes 10649600 | tf_op jit(solution)/shard_map/all_gather | solution.py:18
  12.0 34.8 %all-to-all-start = ((bf16[1024,4,320]{0,2,1:T(8,128)(2,1)}), bf16[1024,4,320]{0,2,1:T(8,128)(2,1)S(1)}, u32[]{:S(2)}, u32[]{:S(2)}) async-start(bf16[1024,4,320]{0,2,1:T(8,128)(2,1)} %tile.2), calls=%async_computation | async-start | bytes 5242880 | tf_op jit(solution)/shard_map/all_to_all | solution.py:24
  16.9 156.6 %reduce-scatter.5.cloned.1.call-start = ((), (), s32[]{:S(2)}) async-start(), calls=%async_computation.4 | async-start | bytes 3276800 | tf_op jit(solution)/shard_map/reduce_scatter | solution.py:38
  113.7 6.1 %copy-start.4 = (f32[1280]{0:T(1024)S(1)}, f32[1280]{0:T(1024)}, u32[]{:S(2)}) copy-start(f32[1280]{0:T(1024)} %param.15) | copy-start | bytes 15364
  119.8 20.6 %copy-start = (s32[16384]{0:T(1024)S(1)}, s32[16384]{0:T(1024)}, u32[]{:S(2)}) copy-start(s32[16384]{0:T(1024)} %param.21) | copy-start | bytes 196612
  140.2 33.3 %copy-start.3 = (f32[320]{0:T(512)S(1)}, f32[320]{0:T(512)}, u32[]{:S(2)}) copy-start(f32[320]{0:T(512)} %param.17) | copy-start | bytes 3844
  140.2 66.4 %reduce-scatter.7.cloned.1.call-start = ((), (), s32[]{:S(2)}) async-start(), calls=%async_computation.6 | async-start | bytes 819200
  175.8 31.9 %copy-start.5 = (f32[320]{0:T(512)S(1)}, f32[320]{0:T(512)}, u32[]{:S(2)}) copy-start(f32[320]{0:T(512)} %param.19) | copy-start | bytes 3844
  209.0 26.5 %all-to-all-start.1 = ((bf16[64,8,320]{2,1,0:T(8,128)(2,1)}), bf16[64,8,320]{2,1,0:T(8,128)(2,1)S(1)}, u32[]{:S(2)}, u32[]{:S(2)}) async-start(bf16[64,8,320]{2,1,0:T(8,128)(2,1)} %bitcast.10), calls=%async_computation.2 | async-start | bytes 786432 | tf_op jit(solution)/shard_map/all_to_all | solution.py:73
Sparse Core Ops, SparseCore 0:
  10.1 90.6 all-gather.3
  140.3 33.0 reduce-scatter.4
  183.7 22.8 reduce-scatter.6
